TPU v7x, 32 devices: a whole 2x2x4 slice. The times are simulated.
32 devices in a mesh: rep: 2 (over x), shard: 16 (over z, y, core).
Axes of the slice: x: 2, y: 2, z: 4, core: 2. Of those that a mesh axis runs over, the one named last changes fastest.
Arguments:
- block_input: bfloat16 [4096, 2048], P(('rep', 'shard')), may hold values from -6 to 6
- out_grad: bfloat16 [4096, 2048], P(('rep', 'shard')), may hold values from -6 to 6
- segments: int32 [32, 128], P(('rep', 'shard')), may hold values from 0 to 2, as said below
- positions: int32 [32, 128], P(('rep', 'shard')), may hold values from 0 to 1023, as said below
- attn_gain: float32 [2048], replicated, may hold values from 0.5 to 1.5
- mlp_gain: float32 [2048], replicated, may hold values from 0.5 to 1.5
- q_gain: float32 [128], replicated, may hold values from 0.5 to 2
- k_gain: float32 [128], replicated, may hold values from 0.5 to 2
- w_q: bfloat16 [2048, 2048], P('shard'), may hold values from -0.125 to 0.125
- key_matrix: bfloat16 [2048, 1024], P('shard'), may hold values from -0.125 to 0.125
- value_matrix: bfloat16 [2048, 1024], P('shard'), may hold values from -0.125 to 0.125
- w_o: bfloat16 [2048, 2048], P('shard'), may hold values from -0.75 to 0.75
- w_gate: bfloat16 [2048, 6144], P('shard'), may hold values from -0.125 to 0.125
- w_up: bfloat16 [2048, 6144], P('shard'), may hold values from -0.125 to 0.125
- w_down: bfloat16 [2048, 6144], P('shard'), may hold values from -0.078125 to 0.078125
Outputs:
- output: bfloat16 [4096, 2048], P(('rep', 'shard'))
- grad_input: float32 [4096, 2048], P(('rep', 'shard'))
- grad_w_q: float32 [2048, 2048], P('shard')
- grad_w_k: float32 [2048, 1024], P('shard')
- grad_w_v: float32 [2048, 1024], P('shard')
- grad_w_o: float32 [2048, 2048], P('shard')
- grad_w_gate: float32 [2048, 6144], P('shard')
- grad_w_up: float32 [2048, 6144], P('shard')
- grad_w_down: float32 [2048, 6144], P('shard')
- grad_attn_gain: float32 [2048], replicated
- grad_mlp_gain: float32 [2048], replicated
- grad_q_gain: float32 [128], replicated
- grad_k_gain: float32 [128], replicated
Inputs may be any that keep to these rules, and one draw needn't show every extreme that they name: `segments`: in each sequence the segment numbers never fall, the first token has 0 and the last has 2. Within a segment the positions rise by one from token to token; segments 1 and 2 start at position 0.
All inputs are finite; a program needn't handle non-finite values.
Results may differ from a plain program's by a relative error of at most 0.015.
Values may be sent and summed in bfloat16 or wider, within the bound.
No kernel may reach another device: no remote copies, remote signals or barrier semaphores. Data moves between devices by JAX's collectives and lax.ppermute only.
A program may use at most 768 MiB of HBM per device.

v0:
```python
import math
import jax
import jax.numpy as jnp
from jax import lax
from jax.sharding import PartitionSpec as P

EPSILON = 1e-06
ROPE_BASE = 1000000.0
NEG_FILL = -1e30


def rope_tables(positions, half):
    freq = jnp.exp(jnp.arange(half, dtype=jnp.float32) * (-math.log(ROPE_BASE) / half))
    angles = positions.reshape(-1).astype(jnp.float32)[:, None, None] * freq
    return (jnp.cos(angles), jnp.sin(angles))


def rotate(vectors, cosine, sine):
    half = vectors.shape[-1] // 2
    first, second = (vectors[..., :half], vectors[..., half:])
    return jnp.concatenate([first * cosine - second * sine, second * cosine + first * sine], -1)


def unrotate(grads, cosine, sine):
    half = grads.shape[-1] // 2
    first, second = (grads[..., :half], grads[..., half:])
    return jnp.concatenate([first * cosine + second * sine, second * cosine - first * sine], -1)


def head_norm(heads, gain):
    recip = lax.rsqrt(jnp.mean(heads * heads, -1, keepdims=True) + EPSILON)
    return (heads * recip * gain, recip)


def norm_back(grads, inputs, recip, gain, axes):
    normal = inputs * recip
    scaled = grads * gain
    gain_grad = jnp.sum(grads * normal, axis=axes)
    input_grad = recip * (scaled - normal * jnp.mean(scaled * normal, -1, keepdims=True))
    return (input_grad, gain_grad)


def attention_mask(segments):
    packed_length = segments.shape[1]
    same = segments[:, :, None] == segments[:, None, :]
    places = jnp.arange(packed_length)
    causal = places[None, :] <= places[:, None]
    return same & causal[None]


def contract_rows(left, right):
    return lax.dot_general(
        left, right, (((0,), (0,)), ((), ())), preferred_element_type=jnp.float32
    )


def contract_cols(left, right):
    return lax.dot_general(
        left, right, (((1,), (1,)), ((), ())), preferred_element_type=jnp.float32
    )


def head_scores(rotated_query_rows, rotated_key_rows, mask, kv_heads, head):
    sequence_list, packed_length = (mask.shape[0], mask.shape[1])
    groups = rotated_query_rows.shape[1] // kv_heads
    query_rows = rotated_query_rows.reshape(sequence_list, packed_length, kv_heads, groups, head)
    every_key_row = rotated_key_rows.reshape(sequence_list, packed_length, kv_heads, head)
    scores = jnp.einsum(
        "slkgd,smkd->skglm", query_rows, every_key_row, preferred_element_type=jnp.float32
    ) * head ** (-0.5)
    return (jnp.where(mask[:, None, None], scores, NEG_FILL), query_rows, every_key_row)


def attend_forward(rotated_query_rows, rotated_key_rows, value_rows, mask):
    sequence_list, packed_length = (mask.shape[0], mask.shape[1])
    kv_heads, head = (value_rows.shape[1], value_rows.shape[2])
    scores, query_rows, every_key_row = head_scores(
        rotated_query_rows, rotated_key_rows, mask, kv_heads, head
    )
    top = jnp.max(scores, -1, keepdims=True)
    expo = jnp.exp(scores - top)
    total = jnp.sum(expo, -1, keepdims=True)
    probs = (expo / total).astype(jnp.bfloat16)
    log_total = top + jnp.log(total)
    value_heads = value_rows.reshape(sequence_list, packed_length, kv_heads, head)
    attended_rows = jnp.einsum(
        "skglm,smkd->slkgd", probs, value_heads, preferred_element_type=jnp.float32
    )
    return (
        attended_rows.reshape(
            sequence_list * packed_length, rotated_query_rows.shape[1] * head
        ).astype(jnp.bfloat16),
        log_total,
    )


def attend_backward(
    rotated_query_rows,
    rotated_key_rows,
    value_rows,
    attended_rows,
    attended_gradient,
    log_total,
    mask,
):
    sequence_list, packed_length = (mask.shape[0], mask.shape[1])
    kv_heads, head = (value_rows.shape[1], value_rows.shape[2])
    groups = rotated_query_rows.shape[1] // kv_heads
    scores, query_rows, every_key_row = head_scores(
        rotated_query_rows, rotated_key_rows, mask, kv_heads, head
    )
    probs_back = jnp.where(mask[:, None, None], jnp.exp(scores - log_total), 0.0)
    output_gradient = attended_gradient.reshape(
        sequence_list, packed_length, kv_heads, groups, head
    )
    value_heads = value_rows.reshape(sequence_list, packed_length, kv_heads, head)
    value_rows_gradient = jnp.einsum(
        "skglm,slkgd->smkd",
        probs_back.astype(jnp.bfloat16),
        output_gradient,
        preferred_element_type=jnp.float32,
    )
    grad_probs = jnp.einsum(
        "slkgd,smkd->skglm", output_gradient, value_heads, preferred_element_type=jnp.float32
    )
    complete_output = attended_rows.reshape(
        sequence_list, packed_length, kv_heads, groups, head
    ).astype(jnp.float32)
    delta = jnp.transpose(
        jnp.sum(output_gradient.astype(jnp.float32) * complete_output, -1), (0, 2, 3, 1)
    )[..., None]
    grad_scores = (probs_back * (grad_probs - delta)).astype(jnp.bfloat16)
    rotated_query_gradient = jnp.einsum(
        "skglm,smkd->slkgd", grad_scores, every_key_row, preferred_element_type=jnp.float32
    ) * head ** (-0.5)
    rotated_key_gradient = jnp.einsum(
        "skglm,slkgd->smkd", grad_scores, query_rows, preferred_element_type=jnp.float32
    ) * head ** (-0.5)
    token_rows = sequence_list * packed_length
    return (
        rotated_query_gradient.reshape(token_rows, rotated_query_rows.shape[1], head),
        rotated_key_gradient.reshape(token_rows, kv_heads, head),
        value_rows_gradient.reshape(token_rows, kv_heads, head),
    )


def on_device(
    block_input,
    out_grad,
    segments,
    positions,
    attn_gain,
    mlp_gain,
    q_gain,
    k_gain,
    w_q,
    key_matrix,
    value_matrix,
    w_o,
    w_gate,
    w_up,
    w_down,
):
    tokens, width = block_input.shape
    head = q_gain.shape[0]
    heads = w_q.shape[1] // head
    kv_heads = key_matrix.shape[1] // head
    hidden = w_gate.shape[1]
    mask = attention_mask(segments)
    cosine, sine = rope_tables(positions, head // 2)
    inputs = block_input.astype(jnp.float32)
    recip_attn = lax.rsqrt(jnp.mean(inputs * inputs, -1, keepdims=True) + EPSILON)
    normed_rows = (inputs * recip_attn * attn_gain).astype(jnp.bfloat16)
    pieces = (
        lax.all_gather(w_q, "shard", axis=0, tiled=True),
        lax.all_gather(key_matrix, "shard", axis=0, tiled=True),
        lax.all_gather(value_matrix, "shard", axis=0, tiled=True),
    )
    columns = normed_rows
    q_proj, k_proj, v_proj = tuple(
        (
            jnp.dot(columns, weight_piece, preferred_element_type=jnp.float32)
            for weight_piece in pieces
        )
    )
    q_heads = q_proj.reshape(tokens, heads, head)
    key_head_rows = k_proj.reshape(tokens, kv_heads, head)
    q_normed, q_recip = head_norm(q_heads, q_gain)
    k_normed, k_recip = head_norm(key_head_rows, k_gain)
    rotated_query_rows = rotate(q_normed, cosine, sine).astype(jnp.bfloat16)
    rotated_key_rows = rotate(k_normed, cosine, sine).astype(jnp.bfloat16)
    value_rows = v_proj.astype(jnp.bfloat16).reshape(tokens, kv_heads, head)
    attended_rows, log_total = attend_forward(
        rotated_query_rows, rotated_key_rows, value_rows, mask
    )
    attn_out = contract_cols(attended_rows, lax.all_gather(w_o, "shard", axis=0, tiled=True))
    mid = inputs + attn_out
    recip_mlp = lax.rsqrt(jnp.mean(mid * mid, -1, keepdims=True) + EPSILON)
    mlp_in = (mid * recip_mlp * mlp_gain).astype(jnp.bfloat16)
    pieces = (
        lax.all_gather(w_gate, "shard", axis=0, tiled=True),
        lax.all_gather(w_up, "shard", axis=0, tiled=True),
    )
    columns = mlp_in
    gate_pre = jnp.dot(columns, pieces[0], preferred_element_type=jnp.float32)
    up_pre = jnp.dot(columns, pieces[1], preferred_element_type=jnp.float32)
    sigma = jax.nn.sigmoid(gate_pre)
    silu_gate = gate_pre * sigma
    act = (silu_gate * up_pre).astype(jnp.bfloat16)
    mlp_out = contract_cols(act, lax.all_gather(w_down, "shard", axis=0, tiled=True))
    output = (mid + mlp_out).astype(jnp.bfloat16)
    grad_top = out_grad.astype(jnp.float32)
    columns = out_grad
    grad_act = jnp.dot(
        columns,
        lax.all_gather(w_down, "shard", axis=0, tiled=True),
        preferred_element_type=jnp.float32,
    )
    grad_gate = (grad_act * up_pre * sigma * (1.0 + gate_pre * (1.0 - sigma))).astype(jnp.bfloat16)
    grad_up = (grad_act * silu_gate).astype(jnp.bfloat16)
    pieces = (
        lax.all_gather(w_gate, "shard", axis=0, tiled=True),
        lax.all_gather(w_up, "shard", axis=0, tiled=True),
    )
    part = contract_cols(grad_gate, pieces[0]) + contract_cols(grad_up, pieces[1])
    grad_mlp_in = part
    mlp_right = jnp.concatenate([grad_gate, grad_up], 1)
    left_in = mlp_in
    left_grad = out_grad
    mlp_grads = lax.psum_scatter(
        jnp.concatenate([contract_rows(left_in, mlp_right), contract_rows(left_grad, act)], 1),
        "shard",
        scatter_dimension=0,
        tiled=True,
    )
    grad_mid_part, mlp_gain_part = norm_back(grad_mlp_in, mid, recip_mlp, mlp_gain, 0)
    grad_mid = grad_top + grad_mid_part
    grad_mid_b = grad_mid.astype(jnp.bfloat16)
    columns = grad_mid_b
    attended_gradient = jnp.dot(
        columns,
        lax.all_gather(w_o, "shard", axis=0, tiled=True),
        preferred_element_type=jnp.float32,
    ).astype(jnp.bfloat16)
    rotated_query_gradient, rotated_key_gradient, value_rows_gradient = attend_backward(
        rotated_query_rows,
        rotated_key_rows,
        value_rows,
        attended_rows,
        attended_gradient,
        log_total,
        mask,
    )
    grad_qh, q_gain_part = norm_back(
        unrotate(rotated_query_gradient, cosine, sine), q_heads, q_recip, q_gain, (0, 1)
    )
    key_heads_gradient, k_gain_part = norm_back(
        unrotate(rotated_key_gradient, cosine, sine), key_head_rows, k_recip, k_gain, (0, 1)
    )
    grad_q = grad_qh.reshape(tokens, heads * head).astype(jnp.bfloat16)
    key_gradient = key_heads_gradient.reshape(tokens, kv_heads * head).astype(jnp.bfloat16)
    value_gradient = value_rows_gradient.reshape(tokens, kv_heads * head).astype(jnp.bfloat16)
    pieces = (
        lax.all_gather(w_q, "shard", axis=0, tiled=True),
        lax.all_gather(key_matrix, "shard", axis=0, tiled=True),
        lax.all_gather(value_matrix, "shard", axis=0, tiled=True),
    )
    part = (
        contract_cols(grad_q, pieces[0])
        + contract_cols(key_gradient, pieces[1])
        + contract_cols(value_gradient, pieces[2])
    )
    attn_right = jnp.concatenate([grad_q, key_gradient, value_gradient], 1)
    left_in = normed_rows
    left_grad = grad_mid_b
    attn_grads = lax.psum_scatter(
        jnp.concatenate(
            [contract_rows(left_in, attn_right), contract_rows(left_grad, attended_rows)], 1
        ),
        "shard",
        scatter_dimension=0,
        tiled=True,
    )
    grad_in_part, attn_gain_part = norm_back(part, inputs, recip_attn, attn_gain, 0)
    grad_input = grad_mid + grad_in_part
    gain_totals = lax.psum(
        (attn_gain_part, mlp_gain_part, q_gain_part, k_gain_part), ("rep", "shard")
    )
    attn_total, mlp_total = (
        lax.psum(attn_grads.astype(jnp.bfloat16), "rep").astype(jnp.float32),
        lax.psum(mlp_grads.astype(jnp.bfloat16), "rep").astype(jnp.float32),
    )
    q_cols = heads * head
    k_cols = kv_heads * head
    grad_w_q = attn_total[:, :q_cols]
    grad_w_k = attn_total[:, q_cols : q_cols + k_cols]
    grad_w_v = attn_total[:, q_cols + k_cols : q_cols + 2 * k_cols]
    grad_w_o = attn_total[:, q_cols + 2 * k_cols :]
    grad_w_gate = mlp_total[:, :hidden]
    grad_w_up = mlp_total[:, hidden : 2 * hidden]
    grad_w_down = mlp_total[:, 2 * hidden :]
    return (
        output,
        grad_input,
        grad_w_q,
        grad_w_k,
        grad_w_v,
        grad_w_o,
        grad_w_gate,
        grad_w_up,
        grad_w_down,
        gain_totals[0],
        gain_totals[1],
        gain_totals[2],
        gain_totals[3],
    )


def solution(mesh):
    placed = (
        P(("rep", "shard"), None),
        P(("rep", "shard"), None),
        P(("rep", "shard"), None),
        P(("rep", "shard"), None),
        P(),
        P(),
        P(),
        P(),
        P("shard", None),
        P("shard", None),
        P("shard", None),
        P("shard", None),
        P("shard", None),
        P("shard", None),
        P("shard", None),
    )
    return jax.shard_map(
        on_device,
        mesh=mesh,
        in_specs=placed,
        out_specs=(
            P(("rep", "shard"), None),
            P(("rep", "shard"), None),
            P("shard", None),
            P("shard", None),
            P("shard", None),
            P("shard", None),
            P("shard", None),
            P("shard", None),
            P("shard", None),
            P(),
            P(),
            P(),
            P(),
        ),
        check_vma=False,
    )
```

profile of v0, /device:TPU:0, one launch (start us, length us, event | category | flops | bytes accessed | tf_op | source)
XLA Modules:
  0.0 2806.3 jit_solution(15419628978582923309)
XLA Ops:
  14.5 49.1 %all-gather.8.cloned.1.call-done = bf16[2048,1024]{1,0:T(8,128)(2,1)} async-done(((bf16[128,1024]{1,0:T(8,128)(2,1)}), bf16[2048,1024]{1,0:T(8,128)(2,1)}) %all-gather.8.cloned.1.call-update) | async-done | bytes 4194320 | tf_op jit(solution)/shard_map/all_gather | solution.py:177
  63.5 2.9 fusion.19
  66.6 48.2 %all-gather.10.cloned.1.call-done = bf16[2048,1024]{1,0:T(8,128)(2,1)} async-done(((bf16[128,1024]{1,0:T(8,128)(2,1)}), bf16[2048,1024]{1,0:T(8,128)(2,1)}) %all-gather.10.cloned.1.call-update) | async-done | bytes 4194320 | tf_op jit(solution)/shard_map/all_gather | solution.py:176
  114.8 2.9 fusion.66
  119.3 71.0 %all-gather.12.cloned.1.call-done = bf16[2048,2048]{1,0:T(8,128)(2,1)} async-done(((bf16[128,2048]{1,0:T(8,128)(2,1)}), bf16[2048,2048]{1,0:T(8,128)(2,1)}) %all-gather.12.cloned.1.call-update) | async-done | bytes 8388624 | tf_op jit(solution)/shard_map/all_gather | solution.py:175
  190.4 4.7 fusion.64
  200.2 65.4 %all-gather.14.cloned.1.call-done = bf16[2048,2048]{1,0:T(8,128)(2,1)} async-done(((bf16[128,2048]{1,0:T(8,128)(2,1)}), bf16[2048,2048]{1,0:T(8,128)(2,1)}) %all-gather.14.cloned.1.call-update) | async-done | bytes 8388624 | tf_op jit(solution)/shard_map/all_gather | solution.py:196
  265.6 6.4 multiply_reduce_fusion.4
  272.8 121.1 %all-gather.18.cloned.1.call-done = bf16[2048,6144]{1,0:T(8,128)(2,1)} async-done(((bf16[128,6144]{1,0:T(8,128)(2,1)}), bf16[2048,6144]{1,0:T(8,128)(2,1)}) %all-gather.18.cloned.1.call-update) | async-done | bytes 25165840 | tf_op jit(solution)/shard_map/all_gather | solution.py:202
  393.9 13.7 fusion.75
  407.6 116.4 %all-gather.16.cloned.1.call-done = bf16[2048,6144]{1,0:T(8,128)(2,1)} async-done(((bf16[128,6144]{1,0:T(8,128)(2,1)}), bf16[2048,6144]{1,0:T(8,128)(2,1)}) %all-gather.16.cloned.1.call-update) | async-done | bytes 25165840 | tf_op jit(solution)/shard_map/all_gather | solution.py:201
  524.0 13.2 fusion.74
  537.2 117.0 %all-gather.20.cloned.1.call-done = bf16[2048,6144]{1,0:T(8,128)(2,1)} async-done(((bf16[128,6144]{1,0:T(8,128)(2,1)}), bf16[2048,6144]{1,0:T(8,128)(2,1)}) %all-gather.20.cloned.1.call-update) | async-done | bytes 25165840 | tf_op jit(solution)/shard_map/all_gather | solution.py:210
  654.2 14.8 multiply_convert_fusion
  668.9 13.5 fusion.76
  682.5 15.2 multiply_reduce_fusion
  700.0 5.8 convolution_convert_fusion
  717.4 8.1 fusion.50
  740.5 13.6 fusion.31
  754.1 33.6 %pad_maximum_fusion.1 = f32[2048,6144]{1,0:T(8,128)} fusion(f32[2048,2048]{1,0:T(8,128)} %fusion.50, f32[2048,4096]{1,0:T(8,128)} %fusion.31), kind=kLoop, calls=%fused_computation.1 | loop fusion | flops 12582912 | bytes 100663296 | tf_op jit(solution)/shard_map/concatenate | solution.py:277
  789.1 32.8 %convolution_bitcast_fusion = f32[2048,6144]{1,0:T(8,128)} fusion(bf16[128,6144]{1,0:T(8,128)(2,1)S(1)} %copy-done.13, bf16[128,2048]{1,0:T(8,128)(2,1)} %param.16), kind=kOutput, calls=%fused_computation.2 | convolution fusion | flops 3221225472 | bytes 52428800 | tf_op jit(solution)/shard_map/dot_general | solution.py:52
  822.0 48.1 %fusion = f32[2048,12288]{1,0:T(8,128)} fusion(bf16[128,2048]{1,0:T(8,128)(2,1)} %copy-done.15, bf16[128,6144]{1,0:T(8,128)(2,1)} %get-tuple-element.25, bf16[128,6144]{1,0:T(8,128)(2,1)S(1)} %copy-done.14), kind=kOutput, calls=%fused_computation.3 | convolution fusion | flops 6448742400 | bytes 104333312 | tf_op jit(solution)/shard_map/dot_general | solution.py:52
  870.1 100.2 %pad_maximum_fusion = f32[2048,18432]{1,0:T(8,128)} fusion(f32[2048,6144]{1,0:T(8,128)} %convolution_bitcast_fusion, f32[2048,12288]{1,0:T(8,128)} %fusion), kind=kLoop, calls=%fused_computation | loop fusion | flops 37748736 | bytes 301989888 | tf_op jit(solution)/shard_map/concatenate | solution.py:231
  970.6 285.1 %reduce-scatter.3.cloned.1.call-done = f32[128,6144]{1,0:T(8,128)} async-done(((f32[2048,6144]{1,0:T(8,128)}), f32[128,6144]{1,0:T(8,128)}) %reduce-scatter.3.cloned.1.call-update) | async-done | bytes 3145744 | tf_op jit(solution)/shard_map/reduce_scatter | solution.py:276
  1255.7 3.2 convert_element_type.156
  1258.9 1370.2 %reduce-scatter.5.cloned.1.call-done = f32[128,18432]{1,0:T(8,128)} async-done(((f32[2048,18432]{1,0:T(8,128)}), f32[128,18432]{1,0:T(8,128)}) %reduce-scatter.5.cloned.1.call-update) | async-done | bytes 9437200 | tf_op jit(solution)/shard_map/reduce_scatter | solution.py:230
  2629.1 6.5 convert_element_type.158
  2636.7 6.4 fusion.77
  2648.2 40.2 %all-reduce = (f32[2048]{0:T(1024)}, f32[2048]{0:T(1024)}, f32[128]{0:T(128)}, f32[128]{0:T(128)}) all-reduce(f32[2048]{0:T(1024)S(1)} %get-tuple-element.15, f32[2048]{0:T(1024)S(1)} %copy-done.50, f32[128]{0:T(128)S(1)} %bitcast_reduce_fusion, f32[128]{0:T(128)S(1)} %bitcast_reduce_fusion.1), channel_id=1, replica_groups=mesh['rep'=2,'shard'=16] {'rep','shard'}, use_global_device_ids=true, to_apply=%region_16.17 | all-reduce | flops 4352 | bytes 34816 | tf_op jit(solution)/shard_map/psum | solution.py:286
  2691.0 14.2 fusion.5
  2705.2 84.7 %all-reduce.4.cloned.1.call-done = (bf16[128,6144]{1,0:T(8,128)(2,1)}, bf16[128,18432]{1,0:T(8,128)(2,1)}) async-done(((bf16[128,6144]{1,0:T(8,128)(2,1)}, bf16[128,18432]{1,0:T(8,128)(2,1)}), (bf16[128,6144]{1,0:T(8,128)(2,1)}, bf16[128,18432]{1,0:T(8,128)(2,1)})) %all-reduce.4.cloned.1.call-update) | async-done | bytes 6291472 | tf_op jit(solution)/shard_map/psum | solution.py:290
  2795.0 4.0 fusion.69
  (203 shorter events, 58.5 us)
Async XLA Ops:
  7.2 6.2 copy-start.58
  7.2 56.3 %copy-start.37 = (f32[2048]{0:T(1024)S(1)}, f32[2048]{0:T(1024)}, u32[]{:S(2)}) copy-start(f32[2048]{0:T(1024)} %param.19) | copy-start | bytes 24580
  7.2 56.3 %all-gather.8.cloned.1.call-start = ((), (), s32[]{:S(2)}) async-start(), calls=%async_computation.2 | async-start | bytes 4456448 | tf_op jit(solution)/shard_map/all_gather | solution.py:177
  8.0 106.8 %all-gather.10.cloned.1.call-start = ((), (), s32[]{:S(2)}) async-start(), calls=%async_computation.3 | async-start | bytes 4456448 | tf_op jit(solution)/shard_map/all_gather | solution.py:176
  8.7 181.6 %all-gather.12.cloned.1.call-start = ((), (), s32[]{:S(2)}) async-start(), calls=%async_computation.4 | async-start | bytes 8912896 | tf_op jit(solution)/shard_map/all_gather | solution.py:175
  9.5 256.1 %all-gather.14.cloned.1.call-start = ((), (), s32[]{:S(2)}) async-start(), calls=%async_computation.5 | async-start | bytes 8912896 | tf_op jit(solution)/shard_map/all_gather | solution.py:196
  10.0 383.8 %all-gather.18.cloned.1.call-start = ((), (), s32[]{:S(2)}) async-start(), calls=%async_computation.7 | async-start | bytes 26738688 | tf_op jit(solution)/shard_map/all_gather | solution.py:202
  10.6 513.3 %all-gather.16.cloned.1.call-start = ((), (), s32[]{:S(2)}) async-start(), calls=%async_computation.6 | async-start | bytes 26738688 | tf_op jit(solution)/shard_map/all_gather | solution.py:201
  11.2 643.0 %all-gather.20.cloned.1.call-start = ((), (), s32[]{:S(2)}) async-start(), calls=%async_computation.8 | async-start | bytes 26738688 | tf_op jit(solution)/shard_map/all_gather | solution.py:210
  12.0 1243.7 %reduce-scatter.3.cloned.1.call-start = ((), (), s32[]{:S(2)}) async-start(), calls=%async_computation.9 | async-start | bytes 53477376 | tf_op jit(solution)/shard_map/reduce_scatter | solution.py:276
  12.2 178.1 %copy-start.46 = (f32[128]{0:T(128)}, f32[128]{0:T(128)S(1)}, u32[]{:S(2)}) copy-start(f32[128]{0:T(128)S(1)} %add_rsqrt_fusion.3) | copy-start | bytes 1540
  66.5 132.4 %copy-start.36 = (bf16[16,8,8,128]{3,2,1,0:T(8,128)(2,1)}, bf16[16,8,8,128]{3,2,1,0:T(8,128)(2,1)S(1)}, u32[]{:S(2)}) copy-start(bf16[16,8,8,128]{3,2,1,0:T(8,128)(2,1)S(1)} %copy.175) | copy-start | bytes 786436
  119.3 78.8 %copy-start.28 = (bf16[128,8,64]{2,0,1:T(8,128)(2,1)}, bf16[128,8,64]{2,0,1:T(8,128)(2,1)S(1)}, u32[]{:S(2)}) copy-start(bf16[128,8,64]{2,0,1:T(8,128)(2,1)S(1)} %get-tuple-element.50) | copy-start | bytes 393220
  198.2 67.4 %copy-start.22 = (bf16[128,16,64]{2,0,1:T(8,128)(2,1)}, bf16[128,16,64]{2,0,1:T(8,128)(2,1)S(1)}, u32[]{:S(2)}) copy-start(bf16[128,16,64]{2,0,1:T(8,128)(2,1)S(1)} %copy.127) | copy-start | bytes 786436
  200.1 71.8 %copy-start.24 = (bf16[8,128,2,128]{3,1,2,0:T(8,128)(2,1)}, bf16[8,128,2,128]{3,1,2,0:T(8,128)(2,1)S(1)}, u32[]{:S(2)}) copy-start(bf16[8,128,2,128]{3,1,2,0:T(8,128)(2,1)S(1)} %convolution_convert_fusion.1) | copy-start | bytes 1572868
  265.6 7.1 copy-start.42
  271.9 426.4 %copy-start.2 = (f32[128,2048]{1,0:T(8,128)}, f32[128,2048]{1,0:T(8,128)S(1)}, u32[]{:S(2)}) copy-start(f32[128,2048]{1,0:T(8,128)S(1)} %get-tuple-element.56) | copy-start | bytes 3145732
  272.0 121.9 %copy-start.54 = (f32[128]{0:T(128)}, f32[128]{0:T(128)S(1)}, u32[]{:S(2)}) copy-start(f32[128]{0:T(128)S(1)} %add_rsqrt_fusion.2) | copy-start | bytes 1540
  272.8 251.1 %copy-start.15 = (bf16[128,2048]{1,0:T(8,128)(2,1)}, bf16[128,2048]{1,0:T(8,128)(2,1)S(1)}, u32[]{:S(2)}) copy-start(bf16[128,2048]{1,0:T(8,128)(2,1)S(1)} %multiply_convert_fusion.3) | copy-start | bytes 1572868
  407.6 246.6 %copy-start.32 = (bf16[128,2048]{1,0:T(8,128)(2,1)S(1)}, bf16[128,2048]{1,0:T(8,128)(2,1)}, u32[]{:S(2)}) copy-start(bf16[128,2048]{1,0:T(8,128)(2,1)} %param.16) | copy-start | bytes 1572868
  700.0 17.4 copy-start.4
  705.8 6.0 copy-start.43
  717.4 8.1 copy-start.30
  737.6 16.4 copy-start.26
  740.5 13.6 copy-start.18
  787.7 1841.4 %reduce-scatter.5.cloned.1.call-start = ((), (), s32[]{:S(2)}) async-start(), calls=%async_computation.10 | async-start | bytes 160432128 | tf_op jit(solution)/shard_map/reduce_scatter | solution.py:230
  789.1 32.8 %copy-start.14 = (bf16[128,6144]{1,0:T(8,128)(2,1)S(1)}, bf16[128,6144]{1,0:T(8,128)(2,1)}, u32[]{:S(2)}) copy-start(bf16[128,6144]{1,0:T(8,128)(2,1)} %get-tuple-element.26) | copy-start | bytes 4718596
  970.3 1819.6 %all-reduce.4.cloned.1.call-start = ((), (), s32[]{:S(2)}) async-start(), calls=%async_computation.11 | async-start | bytes 12582912 | tf_op jit(solution)/shard_map/psum | solution.py:290
  2636.7 6.4 copy-start.12
  2636.7 6.4 copy-start.27
  2645.5 42.9 %copy-start.5 = (f32[128,2048]{1,0:T(8,128)S(1)}, f32[128,2048]{1,0:T(8,128)}, u32[]{:S(2)}) copy-start(f32[128,2048]{1,0:T(8,128)} %copy-done.4) | copy-start | bytes 3145732
  2645.5 45.5 %copy-start.3 = (f32[128,2048]{1,0:T(8,128)S(1)}, f32[128,2048]{1,0:T(8,128)}, u32[]{:S(2)}) copy-start(f32[128,2048]{1,0:T(8,128)} %copy-done.2) | copy-start | bytes 3145732
  (38 other events, 120.0 us)
Sparse Core Ops, SparseCore 0:
  10.2 53.2 all-gather.7
  65.7 49.0 all-gather.9
  116.9 73.3 all-gather.11
  192.4 73.1 all-gather.13
  267.0 126.8 all-gather.17
  395.3 128.5 all-gather.15
  525.5 128.5 all-gather.19
  787.9 467.7 reduce-scatter.2
  1259.9 1369.1 reduce-scatter.4
  2635.8 154.1 all-reduce.3
where the time goes:
time: 2820 us; the launch traced here: 2810 us
  waiting for transfers between devices  2330 us (83%)
  matrix products  227 us (8%)
  other arithmetic  162 us (6%)
  blocking collectives  40.2 us (1%)
  local copies, waits for them, and re-layouts  28.5 us (1%)
    reduce_scatter x1, waiting for transfers between devices, on_device(): lax.psum_scatter(jnp.concatenate([contract_rows(left_in, mlp_right), cont...  1370 us
    reduce_scatter x1, waiting for transfers between devices, on_device(): lax.psum_scatter(jnp.concatenate([contract_rows(left_in, attn_right), con...  285 us
    all_gather x1, waiting for transfers between devices, on_device(): lax.all_gather(w_up, 'shard', axis=0, tiled=True)  121 us
    all_gather x1, waiting for transfers between devices, on_device(): lax.all_gather(w_down, 'shard', axis=0, tiled=True)  117 us
    all_gather x1, waiting for transfers between devices, on_device(): lax.all_gather(w_gate, 'shard', axis=0, tiled=True)  116 us
    dot_general x4, matrix products, contract_rows(): lax.dot_general(left, right, (((0,), (0,)), ((), ())), preferred_element_...  103 us
    concatenate x1, other arithmetic, on_device(): jnp.concatenate([contract_rows(left_in, mlp_right), contract_rows(left_gr...  100 us
    psum x1, waiting for transfers between devices, on_device(): lax.psum(attn_grads.astype(jnp.bfloat16), 'rep').astype(jnp.float32)  84.7 us
  transfers between devices with their start and end apart: 10, of which 10 were waited for; matrix products, arithmetic and copies ran while one was open for 9% of the time, Pallas kernels for 0%

commit v1 on v0

--- a/solution.py
+++ b/solution.py
@@ -7,6 +7,24 @@
 EPSILON = 1e-06
 ROPE_BASE = 1000000.0
 NEG_FILL = -1e30
+
+
+def ring_gather(array, axis, dim):
+    ways, here, step = (lax.axis_size(axis), lax.axis_index(axis), array.shape[dim])
+    dims = [n * ways if d == dim else n for d, n in enumerate(array.shape)]
+    full = lax.dynamic_update_slice_in_dim(
+        jnp.zeros(dims, array.dtype), array, here * step, axis=dim
+    )
+    going_up = going_down = array
+    for far in range(1, ways // 2 + 1):
+        going_up = lax.ppermute(going_up, axis, [(d, (d + 1) % ways) for d in range(ways)])
+        full = lax.dynamic_update_slice_in_dim(full, going_up, (here - far) % ways * step, axis=dim)
+        if 2 * far < ways:
+            going_down = lax.ppermute(going_down, axis, [(d, (d - 1) % ways) for d in range(ways)])
+            full = lax.dynamic_update_slice_in_dim(
+                full, going_down, (here + far) % ways * step, axis=dim
+            )
+    return full
 
 
 def rope_tables(positions, half):
@@ -197,10 +215,7 @@
     mid = inputs + attn_out
     recip_mlp = lax.rsqrt(jnp.mean(mid * mid, -1, keepdims=True) + EPSILON)
     mlp_in = (mid * recip_mlp * mlp_gain).astype(jnp.bfloat16)
-    pieces = (
-        lax.all_gather(w_gate, "shard", axis=0, tiled=True),
-        lax.all_gather(w_up, "shard", axis=0, tiled=True),
-    )
+    pieces = (lax.all_gather(w_gate, "shard", axis=0, tiled=True), ring_gather(w_up, "shard", 0))
     columns = mlp_in
     gate_pre = jnp.dot(columns, pieces[0], preferred_element_type=jnp.float32)
     up_pre = jnp.dot(columns, pieces[1], preferred_element_type=jnp.float32)

time: 2820 us -> 2910 us (1.032)
  starting transfers between devices: 0.64 us -> 133 us
  waiting for transfers between devices: 2330 us -> 2270 us
  local copies, waits for them, and re-layouts: 28.5 us -> 65.8 us
    ppermute x0 -> x15, waiting for transfers between devices: none -> 158 us  [the longest x8 158 us: ring_gather(): lax.ppermute(going_up, axis, [(d, (d + 1) % ways) for d in range(ways)])]
    ppermute x0 -> x15, starting transfers between devices: none -> 133 us  [the longest x8 128 us: ring_gather(): lax.ppermute(going_up, axis, [(d, (d + 1) % ways) for d in range(ways)])]
    all_gather x1, waiting for transfers between devices: 71 us -> 0.01 us  [on_device(): lax.all_gather(w_q, 'shard', axis=0, tiled=True)]
    all_gather x1, waiting for transfers between devices: 49.1 us -> 0.01 us  [on_device(): lax.all_gather(value_matrix, 'shard', axis=0, tiled=True)]
    all_gather x1, waiting for transfers between devices: 48.2 us -> 0.01 us  [on_device(): lax.all_gather(key_matrix, 'shard', axis=0, tiled=True)]
    all_gather x1, waiting for transfers between devices: 65.4 us -> 31.2 us  [on_device(): lax.all_gather(w_o, 'shard', axis=0, tiled=True)]
    dynamic_update_slice x0 -> x16, local copies, waits for them, and re-layouts: none -> 29.1 us  [the longest x8 16 us: ring_gather(): lax.dynamic_update_slice_in_dim(full, going_up, (here - far) % ways * ste...]
  transfers between devices with their start and end apart: 10 -> 25, of which waited for: 10 -> 15; matrix products, arithmetic and copies ran while one was open for 9% -> 11% of each run, Pallas kernels for 0% -> 0%
where the time goes in v1:
time: 2910 us
  waiting for transfers between devices  2270 us (78%)
  matrix products  223 us (8%)
  other arithmetic  162 us (6%)
  starting transfers between devices  133 us (5%)
  local copies, waits for them, and re-layouts  65.8 us (2%)
  blocking collectives  40.2 us (1%)
    reduce_scatter x1, waiting for transfers between devices, on_device(): lax.psum_scatter(jnp.concatenate([contract_rows(left_in, mlp_right), cont...  1370 us
    reduce_scatter x1, waiting for transfers between devices, on_device(): lax.psum_scatter(jnp.concatenate([contract_rows(left_in, attn_right), con...  285 us
    ppermute x8, waiting for transfers between devices, ring_gather(): lax.ppermute(going_up, axis, [(d, (d + 1) % ways) for d in range(ways)])  158 us
    ppermute x8, starting transfers between devices, ring_gather(): lax.ppermute(going_up, axis, [(d, (d + 1) % ways) for d in range(ways)])  128 us
    all_gather x1, waiting for transfers between devices, on_device(): lax.all_gather(w_gate, 'shard', axis=0, tiled=True)  123 us
    all_gather x1, waiting for transfers between devices, on_device(): lax.all_gather(w_down, 'shard', axis=0, tiled=True)  117 us
    dot_general x4, matrix products, contract_rows(): lax.dot_general(left, right, (((0,), (0,)), ((), ())), preferred_element_...  103 us
    concatenate x1, other arithmetic, on_device(): jnp.concatenate([contract_rows(left_in, mlp_right), contract_rows(left_gr...  100 us
  transfers between devices with their start and end apart: 25, of which 15 were waited for; matrix products, arithmetic and copies ran while one was open for 11% of the time, Pallas kernels for 0%

profile of v1, /device:TPU:0, one launch (start us, length us, event | category | flops | bytes accessed | tf_op | source)
XLA Modules:
  0.0 2905.5 jit_solution(8663295006173832211)
XLA Ops:
  18.4 24.6 collective-permute-done
  43.0 13.6 collective-permute-start.2
  75.8 21.4 collective-permute-start.4
  104.0 14.8 collective-permute-done.4
  118.8 26.7 collective-permute-start.6
  149.2 17.3 collective-permute-done.6
  166.5 15.2 collective-permute-start.8
  189.5 14.3 collective-permute-done.8
  203.7 21.4 collective-permute-start.10
  232.1 29.3 %collective-permute-done.10 = bf16[128,6144]{1,0:T(8,128)(2,1)} collective-permute-done((bf16[128,6144]{1,0:T(8,128)(2,1)}, bf16[128,6144]{1,0:T(8,128)(2,1)}, u32[]{:S(2)}, u32[]{:S(2)}) %collective-permute-start.10) | collective-permute-done | bytes 1572896 | tf_op jit(solution)/shard_map/ppermute | solution.py:20
  261.5 18.2 collective-permute-start.12
  285.5 20.7 collective-permute-done.12
  320.6 29.2 %collective-permute-done.14 = bf16[128,6144]{1,0:T(8,128)(2,1)S(1)} collective-permute-done((bf16[128,6144]{1,0:T(8,128)(2,1)S(1)}, bf16[128,6144]{1,0:T(8,128)(2,1)S(1)}, u32[]{:S(2)}, u32[]{:S(2)}) %collective-permute-start.14) | collective-permute-done | bytes 1572896 | tf_op jit(solution)/shard_map/ppermute | solution.py:20
  361.4 31.2 %all-gather.14.cloned.1.call-done = bf16[2048,2048]{1,0:T(8,128)(2,1)} async-done(((bf16[128,2048]{1,0:T(8,128)(2,1)}), bf16[2048,2048]{1,0:T(8,128)(2,1)}) %all-gather.14.cloned.1.call-update) | async-done | bytes 8388624 | tf_op jit(solution)/shard_map/all_gather | solution.py:214
  399.9 122.8 %all-gather.16.cloned.1.call-done = bf16[2048,6144]{1,0:T(8,128)(2,1)} async-done(((bf16[128,6144]{1,0:T(8,128)(2,1)}), bf16[2048,6144]{1,0:T(8,128)(2,1)}) %all-gather.16.cloned.1.call-update) | async-done | bytes 25165840 | tf_op jit(solution)/shard_map/all_gather | solution.py:218
  522.7 13.3 fusion.74
  536.0 116.8 %all-gather.18.cloned.1.call-done = bf16[2048,6144]{1,0:T(8,128)(2,1)} async-done(((bf16[128,6144]{1,0:T(8,128)(2,1)}), bf16[2048,6144]{1,0:T(8,128)(2,1)}) %all-gather.18.cloned.1.call-update) | async-done | bytes 25165840 | tf_op jit(solution)/shard_map/all_gather | solution.py:225
  652.7 11.0 fusion.75
  663.8 13.0 multiply_convert_fusion
  676.8 13.8 fusion.76
  690.6 92.3 %all-gather.20.cloned.1.call-done = bf16[2048,6144]{1,0:T(8,128)(2,1)} async-done(((bf16[128,6144]{1,0:T(8,128)(2,1)}), bf16[2048,6144]{1,0:T(8,128)(2,1)}) %all-gather.20.cloned.1.call-update) | async-done | bytes 25165840 | tf_op jit(solution)/shard_map/all_gather | solution.py:238
  782.9 15.2 multiply_reduce_fusion
  839.7 13.6 fusion.31
  853.3 33.6 %pad_maximum_fusion.1 = f32[2048,6144]{1,0:T(8,128)} fusion(f32[2048,2048]{1,0:T(8,128)} %fusion.50, f32[2048,4096]{1,0:T(8,128)} %fusion.31), kind=kLoop, calls=%fused_computation.1 | loop fusion | flops 12582912 | bytes 100663296 | tf_op jit(solution)/shard_map/concatenate | solution.py:292
  888.3 32.9 %convolution_bitcast_fusion = f32[2048,6144]{1,0:T(8,128)} fusion(bf16[128,6144]{1,0:T(8,128)(2,1)S(1)} %copy-done.13, bf16[128,2048]{1,0:T(8,128)(2,1)} %param.16), kind=kOutput, calls=%fused_computation.2 | convolution fusion | flops 3221225472 | bytes 52428800 | tf_op jit(solution)/shard_map/dot_general | solution.py:70
  921.2 48.1 %fusion = f32[2048,12288]{1,0:T(8,128)} fusion(bf16[128,2048]{1,0:T(8,128)(2,1)} %copy-done.18, bf16[128,6144]{1,0:T(8,128)(2,1)} %get-tuple-element.25, bf16[128,6144]{1,0:T(8,128)(2,1)S(1)} %copy-done.14), kind=kOutput, calls=%fused_computation.3 | convolution fusion | flops 6448742400 | bytes 104333312 | tf_op jit(solution)/shard_map/dot_general | solution.py:70
  969.3 100.3 %pad_maximum_fusion = f32[2048,18432]{1,0:T(8,128)} fusion(f32[2048,6144]{1,0:T(8,128)} %convolution_bitcast_fusion, f32[2048,12288]{1,0:T(8,128)} %fusion), kind=kLoop, calls=%fused_computation | loop fusion | flops 37748736 | bytes 301989888 | tf_op jit(solution)/shard_map/concatenate | solution.py:246
  1069.9 285.0 %reduce-scatter.3.cloned.1.call-done = f32[128,6144]{1,0:T(8,128)} async-done(((f32[2048,6144]{1,0:T(8,128)}), f32[128,6144]{1,0:T(8,128)}) %reduce-scatter.3.cloned.1.call-update) | async-done | bytes 3145744 | tf_op jit(solution)/shard_map/reduce_scatter | solution.py:291
  1358.1 1370.2 %reduce-scatter.5.cloned.1.call-done = f32[128,18432]{1,0:T(8,128)} async-done(((f32[2048,18432]{1,0:T(8,128)}), f32[128,18432]{1,0:T(8,128)}) %reduce-scatter.5.cloned.1.call-update) | async-done | bytes 9437200 | tf_op jit(solution)/shard_map/reduce_scatter | solution.py:245
  2747.3 40.2 %all-reduce = (f32[2048]{0:T(1024)}, f32[2048]{0:T(1024)}, f32[128]{0:T(128)}, f32[128]{0:T(128)}) all-reduce(f32[2048]{0:T(1024)S(1)} %get-tuple-element.15, f32[2048]{0:T(1024)S(1)} %copy-done.53, f32[128]{0:T(128)S(1)} %bitcast_reduce_fusion, f32[128]{0:T(128)S(1)} %bitcast_reduce_fusion.1), channel_id=1, replica_groups=mesh['rep'=2,'shard'=16] {'rep','shard'}, use_global_device_ids=true, to_apply=%region_16.17 | all-reduce | flops 4352 | bytes 34816 | tf_op jit(solution)/shard_map/psum | solution.py:301
  2790.2 14.2 fusion.5
  2804.4 84.8 %all-reduce.4.cloned.1.call-done = (bf16[128,6144]{1,0:T(8,128)(2,1)}, bf16[128,18432]{1,0:T(8,128)(2,1)}) async-done(((bf16[128,6144]{1,0:T(8,128)(2,1)}, bf16[128,18432]{1,0:T(8,128)(2,1)}), (bf16[128,6144]{1,0:T(8,128)(2,1)}, bf16[128,18432]{1,0:T(8,128)(2,1)})) %all-reduce.4.cloned.1.call-update) | async-done | bytes 6291472 | tf_op jit(solution)/shard_map/psum | solution.py:305
  (256 shorter events, 171.1 us)
Async XLA Ops:
  7.2 50.0 %copy-start.61 = (s32[1,128]{1,0:T(1,128)S(1)}, s32[1,128]{1,0:T(1,128)}, u32[]{:S(2)}) copy-start(s32[1,128]{1,0:T(1,128)} %param.17) | copy-start | bytes 1540
  7.2 178.5 %all-gather.8.cloned.1.call-start = ((), (), s32[]{:S(2)}) async-start(), calls=%async_computation.2 | async-start | bytes 4456448 | tf_op jit(solution)/shard_map/all_gather | solution.py:195
  8.0 217.1 %all-gather.10.cloned.1.call-start = ((), (), s32[]{:S(2)}) async-start(), calls=%async_computation.3 | async-start | bytes 4456448 | tf_op jit(solution)/shard_map/all_gather | solution.py:194
  8.7 342.4 %all-gather.12.cloned.1.call-start = ((), (), s32[]{:S(2)}) async-start(), calls=%async_computation.4 | async-start | bytes 8912896 | tf_op jit(solution)/shard_map/all_gather | solution.py:193
  9.5 383.1 %all-gather.14.cloned.1.call-start = ((), (), s32[]{:S(2)}) async-start(), calls=%async_computation.5 | async-start | bytes 8912896 | tf_op jit(solution)/shard_map/all_gather | solution.py:214
  10.0 512.6 %all-gather.16.cloned.1.call-start = ((), (), s32[]{:S(2)}) async-start(), calls=%async_computation.6 | async-start | bytes 26738688 | tf_op jit(solution)/shard_map/all_gather | solution.py:218
  10.6 642.1 %all-gather.18.cloned.1.call-start = ((), (), s32[]{:S(2)}) async-start(), calls=%async_computation.7 | async-start | bytes 26738688 | tf_op jit(solution)/shard_map/all_gather | solution.py:225
  11.2 771.7 %all-gather.20.cloned.1.call-start = ((), (), s32[]{:S(2)}) async-start(), calls=%async_computation.8 | async-start | bytes 26738688 | tf_op jit(solution)/shard_map/all_gather | solution.py:238
  12.0 1342.9 %reduce-scatter.3.cloned.1.call-start = ((), (), s32[]{:S(2)}) async-start(), calls=%async_computation.9 | async-start | bytes 53477376 | tf_op jit(solution)/shard_map/reduce_scatter | solution.py:291
  12.0 30.9 %collective-permute-start = (bf16[128,6144]{1,0:T(8,128)(2,1)S(1)}, bf16[128,6144]{1,0:T(8,128)(2,1)}, u32[]{:S(2)}, u32[]{:S(2)}) collective-permute-start(bf16[128,6144]{1,0:T(8,128)(2,1)S(1)} %copy-done.17), channel_id=1, source_target_pairs={{0,1},{1,2},{2,3},{3,4},{4,5},{5,6},{6,7},{7,8},{8,9},{9,10},{10,1... | collective-permute-start | bytes 4718600 | tf_op jit(solution)/shard_map/ppermute | solution.py:20
  12.5 44.0 %collective-permute-start.1 = (bf16[128,6144]{1,0:T(8,128)(2,1)S(1)}, bf16[128,6144]{1,0:T(8,128)(2,1)}, u32[]{:S(2)}, u32[]{:S(2)}) collective-permute-start(bf16[128,6144]{1,0:T(8,128)(2,1)S(1)} %copy-done.17), channel_id=1, source_target_pairs={{0,15},{1,0},{2,1},{3,2},{4,3},{5,4},{6,5},{7,6},{8,7},{9,8},{10,9... | collective-permute-start | bytes 4718600 | tf_op jit(solution)/shard_map/ppermute | solution.py:23
  43.0 32.8 %collective-permute-start.2 = (bf16[128,6144]{1,0:T(8,128)(2,1)}, bf16[128,6144]{1,0:T(8,128)(2,1)S(1)}, u32[]{:S(2)}, u32[]{:S(2)}) collective-permute-start(bf16[128,6144]{1,0:T(8,128)(2,1)} %collective-permute-done), channel_id=1, source_target_pairs={{0,1},{1,2},{2,3},{3,4},{4,5},{5,6},{6,7},{7,8},{8,9},{9,10},{10,1... | collective-permute-start | bytes 4718600 | tf_op jit(solution)/shard_map/ppermute | solution.py:20
  56.6 40.7 %collective-permute-start.3 = (bf16[128,6144]{1,0:T(8,128)(2,1)}, bf16[128,6144]{1,0:T(8,128)(2,1)S(1)}, u32[]{:S(2)}, u32[]{:S(2)}) collective-permute-start(bf16[128,6144]{1,0:T(8,128)(2,1)} %collective-permute-done.1), channel_id=1, source_target_pairs={{0,15},{1,0},{2,1},{3,2},{4,3},{5,4},{6,5},{7,6},{8,7},{9,8},{10,9... | collective-permute-start | bytes 4718600 | tf_op jit(solution)/shard_map/ppermute | solution.py:23
  56.6 294.5 %copy-start.49 = (f32[128]{0:T(128)}, f32[128]{0:T(128)S(1)}, u32[]{:S(2)}) copy-start(f32[128]{0:T(128)S(1)} %add_rsqrt_fusion.3) | copy-start | bytes 1540
  75.8 43.0 %collective-permute-start.4 = (bf16[128,6144]{1,0:T(8,128)(2,1)S(1)}, bf16[128,6144]{1,0:T(8,128)(2,1)S(1)}, u32[]{:S(2)}, u32[]{:S(2)}) collective-permute-start(bf16[128,6144]{1,0:T(8,128)(2,1)S(1)} %collective-permute-done.2), channel_id=1, source_target_pairs={{0,1},{1,2},{2,3},{3,4},{4,5},{5,6},{6,7},{7,8},{8,9},{9,10},{10,1... | collective-permute-start | bytes 4718600 | tf_op jit(solution)/shard_map/ppermute | solution.py:20
  97.2 48.2 %collective-permute-start.5 = (bf16[128,6144]{1,0:T(8,128)(2,1)S(1)}, bf16[128,6144]{1,0:T(8,128)(2,1)S(1)}, u32[]{:S(2)}, u32[]{:S(2)}) collective-permute-start(bf16[128,6144]{1,0:T(8,128)(2,1)S(1)} %collective-permute-done.3), channel_id=1, source_target_pairs={{0,15},{1,0},{2,1},{3,2},{4,3},{5,4},{6,5},{7,6},{8,7},{9,8},{10,9... | collective-permute-start | bytes 4718600 | tf_op jit(solution)/shard_map/ppermute | solution.py:23
  118.8 47.8 %collective-permute-start.6 = (bf16[128,6144]{1,0:T(8,128)(2,1)S(1)}, bf16[128,6144]{1,0:T(8,128)(2,1)}, u32[]{:S(2)}, u32[]{:S(2)}) collective-permute-start(bf16[128,6144]{1,0:T(8,128)(2,1)S(1)} %collective-permute-done.4), channel_id=1, source_target_pairs={{0,1},{1,2},{2,3},{3,4},{4,5},{5,6},{6,7},{7,8},{8,9},{9,10},{10,1... | collective-permute-start | bytes 4718600 | tf_op jit(solution)/shard_map/ppermute | solution.py:20
  145.4 36.3 %collective-permute-start.7 = (bf16[128,6144]{1,0:T(8,128)(2,1)S(1)}, bf16[128,6144]{1,0:T(8,128)(2,1)S(1)}, u32[]{:S(2)}, u32[]{:S(2)}) collective-permute-start(bf16[128,6144]{1,0:T(8,128)(2,1)S(1)} %collective-permute-done.5), channel_id=1, source_target_pairs={{0,15},{1,0},{2,1},{3,2},{4,3},{5,4},{6,5},{7,6},{8,7},{9,8},{10,9... | collective-permute-start | bytes 4718600 | tf_op jit(solution)/shard_map/ppermute | solution.py:23
  166.5 37.2 %collective-permute-start.8 = (bf16[128,6144]{1,0:T(8,128)(2,1)}, bf16[128,6144]{1,0:T(8,128)(2,1)}, u32[]{:S(2)}, u32[]{:S(2)}) collective-permute-start(bf16[128,6144]{1,0:T(8,128)(2,1)} %collective-permute-done.6), channel_id=1, source_target_pairs={{0,1},{1,2},{2,3},{3,4},{4,5},{5,6},{6,7},{7,8},{8,9},{9,10},{10,1... | collective-permute-start | bytes 4718600 | tf_op jit(solution)/shard_map/ppermute | solution.py:20
  181.7 47.5 %collective-permute-start.9 = (bf16[128,6144]{1,0:T(8,128)(2,1)S(1)}, bf16[128,6144]{1,0:T(8,128)(2,1)}, u32[]{:S(2)}, u32[]{:S(2)}) collective-permute-start(bf16[128,6144]{1,0:T(8,128)(2,1)S(1)} %collective-permute-done.7), channel_id=1, source_target_pairs={{0,15},{1,0},{2,1},{3,2},{4,3},{5,4},{6,5},{7,6},{8,7},{9,8},{10,9... | collective-permute-start | bytes 4718600 | tf_op jit(solution)/shard_map/ppermute | solution.py:23
  203.7 57.7 %collective-permute-start.10 = (bf16[128,6144]{1,0:T(8,128)(2,1)}, bf16[128,6144]{1,0:T(8,128)(2,1)}, u32[]{:S(2)}, u32[]{:S(2)}) collective-permute-start(bf16[128,6144]{1,0:T(8,128)(2,1)} %collective-permute-done.8), channel_id=1, source_target_pairs={{0,1},{1,2},{2,3},{3,4},{4,5},{5,6},{6,7},{7,8},{8,9},{9,10},{10,1... | collective-permute-start | bytes 4718600 | tf_op jit(solution)/shard_map/ppermute | solution.py:20
  228.4 51.2 %copy-start.47 = (f32[128,8]{0,1:T(8,128)}, f32[128,8]{0,1:T(8,128)S(1)}, u32[]{:S(2)}) copy-start(f32[128,8]{0,1:T(8,128)S(1)} %add_rsqrt_fusion.1) | copy-start | bytes 12292
  229.2 53.6 %collective-permute-start.11 = (bf16[128,6144]{1,0:T(8,128)(2,1)}, bf16[128,6144]{1,0:T(8,128)(2,1)S(1)}, u32[]{:S(2)}, u32[]{:S(2)}) collective-permute-start(bf16[128,6144]{1,0:T(8,128)(2,1)} %collective-permute-done.9), channel_id=1, source_target_pairs={{0,15},{1,0},{2,1},{3,2},{4,3},{5,4},{6,5},{7,6},{8,7},{9,8},{10,9... | collective-permute-start | bytes 4718600 | tf_op jit(solution)/shard_map/ppermute | solution.py:23
  261.5 44.8 %collective-permute-start.12 = (bf16[128,6144]{1,0:T(8,128)(2,1)}, bf16[128,6144]{1,0:T(8,128)(2,1)S(1)}, u32[]{:S(2)}, u32[]{:S(2)}) collective-permute-start(bf16[128,6144]{1,0:T(8,128)(2,1)} %collective-permute-done.10), channel_id=1, source_target_pairs={{0,1},{1,2},{2,3},{3,4},{4,5},{5,6},{6,7},{7,8},{8,9},{9,10},{10,1... | collective-permute-start | bytes 4718600 | tf_op jit(solution)/shard_map/ppermute | solution.py:20
  279.9 79.5 %copy-start.32 = (bf16[128,8,64]{2,0,1:T(8,128)(2,1)}, bf16[128,8,64]{2,0,1:T(8,128)(2,1)S(1)}, u32[]{:S(2)}) copy-start(bf16[128,8,64]{2,0,1:T(8,128)(2,1)S(1)} %get-tuple-element.50) | copy-start | bytes 393220
  282.8 36.6 %collective-permute-start.13 = (bf16[128,6144]{1,0:T(8,128)(2,1)S(1)}, bf16[128,6144]{1,0:T(8,128)(2,1)S(1)}, u32[]{:S(2)}, u32[]{:S(2)}) collective-permute-start(bf16[128,6144]{1,0:T(8,128)(2,1)S(1)} %collective-permute-done.11), channel_id=1, source_target_pairs={{0,15},{1,0},{2,1},{3,2},{4,3},{5,4},{6,5},{7,6},{8,7},{9,8},{10,9... | collective-permute-start | bytes 4718600 | tf_op jit(solution)/shard_map/ppermute | solution.py:23
  306.3 43.6 %collective-permute-start.14 = (bf16[128,6144]{1,0:T(8,128)(2,1)S(1)}, bf16[128,6144]{1,0:T(8,128)(2,1)S(1)}, u32[]{:S(2)}, u32[]{:S(2)}) collective-permute-start(bf16[128,6144]{1,0:T(8,128)(2,1)S(1)} %collective-permute-done.12), channel_id=1, source_target_pairs={{0,1},{1,2},{2,3},{3,4},{4,5},{5,6},{6,7},{7,8},{8,9},{9,10},{10,1... | collective-permute-start | bytes 4718600 | tf_op jit(solution)/shard_map/ppermute | solution.py:20
  399.0 399.8 %copy-start.2 = (f32[128,2048]{1,0:T(8,128)}, f32[128,2048]{1,0:T(8,128)S(1)}, u32[]{:S(2)}) copy-start(f32[128,2048]{1,0:T(8,128)S(1)} %get-tuple-element.56) | copy-start | bytes 3145732
  399.9 263.9 %copy-start.18 = (bf16[128,2048]{1,0:T(8,128)(2,1)}, bf16[128,2048]{1,0:T(8,128)(2,1)S(1)}, u32[]{:S(2)}) copy-start(bf16[128,2048]{1,0:T(8,128)(2,1)S(1)} %multiply_convert_fusion.3) | copy-start | bytes 1572868
  399.9 252.9 %copy-start.19 = (bf16[128,2048]{1,0:T(8,128)(2,1)S(1)}, bf16[128,2048]{1,0:T(8,128)(2,1)}, u32[]{:S(2)}) copy-start(bf16[128,2048]{1,0:T(8,128)(2,1)} %param.16) | copy-start | bytes 1572868
  886.9 1841.4 %reduce-scatter.5.cloned.1.call-start = ((), (), s32[]{:S(2)}) async-start(), calls=%async_computation.10 | async-start | bytes 160432128 | tf_op jit(solution)/shard_map/reduce_scatter | solution.py:245
  1069.6 1819.5 %all-reduce.4.cloned.1.call-start = ((), (), s32[]{:S(2)}) async-start(), calls=%async_computation.11 | async-start | bytes 12582912 | tf_op jit(solution)/shard_map/psum | solution.py:305
  (56 other events, 560.7 us)
Sparse Core Ops, SparseCore 0:
  10.2 81.3 all-gather.7
  93.8 82.4 all-gather.9
  178.4 111.1 all-gather.11
  291.6 100.9 all-gather.13
  394.1 128.5 all-gather.15
  524.1 128.5 all-gather.17
  654.3 128.5 all-gather.19
  887.0 467.7 reduce-scatter.2
  1359.1 1369.1 reduce-scatter.4
  2734.9 154.1 all-reduce.3
